TPU v7x, 256 devices: a whole 4x4x8 slice. The times are simulated.
256 devices in a mesh: coil: 32 (over z, y), slab: 8 (over x, core).
Axes of the slice: x: 4, y: 4, z: 8, core: 2. Of those that a mesh axis runs over, the one named last changes fastest.
Arguments:
- cotangent: float32 [32, 2, 256, 256], P('coil', None, 'slab'), may hold values from -60 to 60
- saved_solution: float32 [32, 2, 256, 256], P('coil', None, 'slab'), may hold values from -6 to 6
- coil_maps: bfloat16 [32, 32, 2, 256, 256], P('coil', None, None, 'slab'), may hold values from -1.5 to 1.5
- kspace: bfloat16 [32, 32, 2, 256, 256], P('coil', None, None, 'slab'), may hold values from -6 to 6
- mask_logit: float32 [32, 256], P(None, 'slab'), may hold values from -4.5 to 4.5
- reach: int32 [32, 256], P(None, 'slab'), may hold values from 0 to 256, as said below
Outputs:
- image_grad: float32 [32, 2, 256, 256], P('coil', None, 'slab')
- kspace_grad: bfloat16 [32, 32, 2, 256, 256], P('coil', None, None, 'slab')
- logit_grad: float32 [32, 256], P(None, 'slab')
Inputs may be any that keep to these rules, and one draw needn't show every extreme that they name: reach[z, y] is 0 (line not acquired) or between 128 and 256; line [0, 0] is always fully acquired and line [0, 128] never.
All inputs are finite; a program needn't handle non-finite values.
Results may differ from a plain program's by a relative error of at most 0.02.
Values may be sent and summed in bfloat16 or wider, within the bound.
A program may use at most 64 MiB of HBM per device.

v0:
```python
import math
import jax
import jax.numpy as jnp
from jax import lax
from jax.sharding import PartitionSpec as P

NX = 256
NY = 256
NZ = 32
ITERS = 2
DAMPING = 0.2


def dft_table(length, sign):
    index = jnp.arange(length, dtype=jnp.int32)
    phase = (index[:, None] * index[None, :] % length).astype(jnp.float32) * (
        2.0 * math.pi / length
    )
    factor = 1.0 / math.sqrt(length)
    cosine = jnp.cos(phase) * factor
    sine = sign * jnp.sin(phase) * factor
    table = jnp.stack(
        [jnp.stack([cosine, sine], axis=1), jnp.stack([-sine, cosine], axis=1)], axis=0
    )
    return table.astype(jnp.bfloat16)


def complex_product(factor, operand):
    factor_re, factor_im = (factor[:, 0], factor[:, 1])
    operand_re, operand_im = (operand[:, 0], operand[:, 1])
    return jnp.stack(
        [
            factor_re * operand_re - factor_im * operand_im,
            factor_re * operand_im + factor_im * operand_re,
        ],
        axis=1,
    )


def conjugate_product(factor, operand):
    factor_re, factor_im = (factor[:, 0], factor[:, 1])
    operand_re, operand_im = (operand[:, 0], operand[:, 1])
    return jnp.stack(
        [
            factor_re * operand_re + factor_im * operand_im,
            factor_re * operand_im - factor_im * operand_re,
        ],
        axis=1,
    )


def shards(cotangent, saved_solution, coil_maps, kspace, mask_logit, reach):
    y_fwd, y_inv = (dft_table(NY, -1.0), dft_table(NY, 1.0))
    z_fwd, z_inv = (dft_table(NZ, -1.0), dft_table(NZ, 1.0))
    x_fwd, x_inv = (dft_table(NX, -1.0), dft_table(NX, 1.0))
    maps = coil_maps[0]
    data = kspace[0].astype(jnp.float32)
    readout = jnp.arange(NX, dtype=jnp.int32)
    centred = (readout + NX // 2) % NX
    sampled = (centred[None, None, :] >= (NX - reach)[:, :, None]).astype(jnp.float32)
    gate = jax.nn.sigmoid(mask_logit)
    weight = sampled * gate[:, :, None]
    squared = (weight * weight)[:, None]

    def front(piece):
        product = complex_product(maps.astype(jnp.float32), piece.astype(jnp.float32)).astype(
            jnp.bfloat16
        )
        return jnp.einsum(
            "zixn,inok->zoxk", product, y_fwd, preferred_element_type=jnp.float32
        ).astype(jnp.bfloat16)

    def gathered_front(shard):
        return front(lax.all_gather(shard, "coil", axis=0, tiled=True))

    def to_kspace(rows):
        mixed = jnp.einsum(
            "nixk,inom->moxk", rows, z_fwd, preferred_element_type=jnp.float32
        ).astype(jnp.bfloat16)
        swapped = lax.all_to_all(mixed, "slab", split_axis=3, concat_axis=2, tiled=True)
        return jnp.einsum("zink,inoq->zokq", swapped, x_fwd, preferred_element_type=jnp.float32)

    direction = cotangent
    both = ("coil", "slab")
    saved_k = to_kspace(gathered_front(saved_solution.astype(jnp.bfloat16)))
    first_k = to_kspace(gathered_front(direction.astype(jnp.bfloat16)))
    first_w = weight[:, None] * first_k
    norm_now, first_energy = lax.psum(
        (jnp.sum(direction * direction), jnp.sum(first_w * first_w)), both
    )
    apply_spectrum = (squared * first_k).astype(jnp.bfloat16)
    to_mixed = jnp.einsum(
        "zikq,iqon->zonk", apply_spectrum, x_inv, preferred_element_type=jnp.float32
    ).astype(jnp.bfloat16)
    to_swapped = lax.all_to_all(to_mixed, "slab", split_axis=2, concat_axis=3, tiled=True)
    apply_image_rows = jnp.einsum(
        "mixk,imon->noxk", to_swapped, z_inv, preferred_element_type=jnp.float32
    ).astype(jnp.bfloat16)
    image = jnp.einsum(
        "zixk,ikon->zoxn", apply_image_rows, y_inv, preferred_element_type=jnp.float32
    )
    summed = lax.psum_scatter(
        conjugate_product(maps.astype(jnp.float32), image).astype(jnp.bfloat16),
        "coil",
        scatter_dimension=0,
        tiled=True,
    ).astype(jnp.float32)
    image = summed + DAMPING * direction
    alpha = norm_now / (first_energy + DAMPING * norm_now)
    residual = direction - alpha * image
    second_k = to_kspace(gathered_front(residual.astype(jnp.bfloat16)))
    second_w = weight[:, None] * second_k
    gain = gate * (1.0 - gate)
    target = data - 2.0 * weight[:, None] * saved_k

    def line_terms(spectrum):
        return gain * jnp.sum(sampled * jnp.sum(spectrum * target, axis=1), axis=2)

    norm_next, crossing, second_energy, mixed_energy = lax.psum(
        (
            jnp.sum(residual * residual),
            jnp.sum(residual * direction),
            jnp.sum(second_w * second_w),
            jnp.sum(second_w * first_w),
        ),
        both,
    )
    lines = lax.psum(jnp.stack([line_terms(first_k), line_terms(second_k)]), "coil")
    beta = norm_next / norm_now
    curvature = (
        second_energy
        + beta * (2.0 * mixed_energy + beta * first_energy)
        + DAMPING * (norm_next + beta * (2.0 * crossing + beta * norm_now))
    )
    later = norm_next / curvature
    early = alpha + later * beta
    image_grad = DAMPING * (early * direction + later * residual)
    kspace_grad = (early * first_w + later * second_w).astype(jnp.bfloat16)[None]
    logit_grad = early * lines[0] + later * lines[1]
    return (image_grad, kspace_grad, logit_grad)


def solution(mesh):
    placed = (
        P("coil", None, "slab", None),
        P("coil", None, "slab", None),
        P("coil", None, None, "slab", None),
        P("coil", None, None, "slab", None),
        P(None, "slab"),
        P(None, "slab"),
    )
    return jax.shard_map(
        shards,
        mesh=mesh,
        in_specs=placed,
        out_specs=(
            P("coil", None, "slab", None),
            P("coil", None, None, "slab", None),
            P(None, "slab"),
        ),
        check_vma=False,
    )
```

profile of v0, /device:TPU:2, one launch (start us, length us, event | category | flops | bytes accessed | tf_op | source)
XLA Modules:
  0.0 753.5 jit_solution(7913596652548034315)
XLA Ops:
  7.2 2.1 fusion.89
  14.3 1.8 bitcast_convert_fusion.8
  16.2 74.3 %all-gather.4.cloned.1.call-done = bf16[32,2,32,256]{3,2,1,0:T(8,128)(2,1)} async-done(((bf16[1,2,32,256]{3,2,1,0:T(8,128)(2,1)}), bf16[32,2,32,256]{3,2,1,0:T(8,128)(2,1)}) %all-gather.4.cloned.1.call-update) | async-done | bytes 1048592 | tf_op jit(solution)/shard_map/all_gather | solution.py:74
  90.6 1.8 copy_convert_fusion.2
  93.9 3.2 fusion.4
  97.1 7.2 copy.81
  104.3 7.8 %reshape.272 = bf16[8,2,32768]{2,1,0:T(2,128)(2,1)} reshape(bf16[256,2,32,32]{3,2,1,0:T(8,128)(2,1)} %bitcast.296) | data formatting | bytes 2097152
  112.2 5.5 all-to-all-start
  120.4 11.7 %all-to-all-done = bf16[8,2,32768]{2,1,0:T(2,128)(2,1)} async-done(((bf16[8,2,32768]{2,1,0:T(2,128)(2,1)}), bf16[8,2,32768]{2,1,0:T(2,128)(2,1)}, u32[]{:S(2)}, u32[]{:S(2)}) %all-to-all-start) | async-done | bytes 1048608 | tf_op jit(solution)/shard_map/all_to_all | solution.py:80
  132.1 7.0 reshape.273
  139.1 6.7 copy.82
  145.9 6.2 reshape.243
  152.0 4.4 fusion.2
  158.1 7.2 copy.85
  165.3 7.8 %reshape.274 = bf16[8,2,32768]{2,1,0:T(2,128)(2,1)} reshape(bf16[256,2,32,32]{3,2,1,0:T(8,128)(2,1)} %bitcast.297) | data formatting | bytes 2097152
  173.2 5.6 all-to-all-start.1
  178.9 3.2 copy_convert_fusion
  182.1 11.2 %all-to-all-done.1 = bf16[8,2,32768]{2,1,0:T(2,128)(2,1)} async-done(((bf16[8,2,32768]{2,1,0:T(2,128)(2,1)}), bf16[8,2,32768]{2,1,0:T(2,128)(2,1)}, u32[]{:S(2)}, u32[]{:S(2)}) %all-to-all-start.1) | async-done | bytes 1048608 | tf_op jit(solution)/shard_map/all_to_all | solution.py:95
  193.3 7.0 reshape.275
  200.4 6.9 copy.160
  207.2 6.2 all_to_all.59
  213.4 2.2 fusion.5
  217.2 1.9 subtract_convert_fusion
  221.5 73.8 %all-reduce.2 = (f32[]{:T(128)}, f32[]{:T(128)}) all-reduce(f32[]{:T(128)} %get-tuple-element.49, f32[]{:T(128)} %get-tuple-element.40), channel_id=1, replica_groups=mesh['coil'=32,'slab'=8] {'coil','slab'}, use_global_device_ids=true, to_apply=%region_1.2 | all-reduce | flops 2 | bytes 16 | tf_op jit(solution)/shard_map/psum | solution.py:88
  297.2 71.0 %all-reduce.5.cloned.1.call-done = bf16[32,2,32,256]{3,2,0,1:T(8,128)(2,1)} async-done(((bf16[32,2,32,256]{3,2,0,1:T(8,128)(2,1)}), bf16[32,2,32,256]{3,2,0,1:T(8,128)(2,1)}) %all-reduce.5.cloned.1.call-update) | async-done | bytes 1048592
  368.2 2.7 fusion.61
  370.9 3.3 fusion.7
  374.1 7.2 copy.103
  381.4 7.8 %reshape.278 = bf16[8,2,32768]{2,1,0:T(2,128)(2,1)} reshape(bf16[256,2,32,32]{3,2,1,0:T(8,128)(2,1)} %bitcast.298) | data formatting | bytes 2097152
  389.2 5.1 all-to-all-start.3
  394.3 50.5 %all-gather.6.cloned.1.call-done = bf16[32,2,32,256]{3,2,1,0:T(8,128)(2,1)} async-done(((bf16[1,2,32,256]{3,2,1,0:T(8,128)(2,1)}), bf16[32,2,32,256]{3,2,1,0:T(8,128)(2,1)}) %all-gather.6.cloned.1.call-update) | async-done | bytes 1048592 | tf_op jit(solution)/shard_map/all_gather | solution.py:74
  448.2 2.3 fusion.6
  450.5 6.5 copy.97
  457.0 7.8 %reshape.276 = bf16[8,2,32768]{2,1,0:T(2,128)(2,1)} reshape(bf16[256,2,32,32]{3,2,1,0:T(8,128)(2,1)} %bitcast.299) | data formatting | bytes 2097152
  464.8 4.8 all-to-all-start.2
  469.6 7.0 reshape.279
  476.6 6.7 copy.104
  483.3 5.4 reshape.264
  488.7 3.4 fusion
  492.1 7.0 reshape.277
  499.1 6.7 copy.98
  505.8 6.3 reshape.258
  512.1 6.2 multiply_reduce_fusion
  518.3 74.5 %all-reduce.1 = (f32[]{:T(128)}, f32[]{:T(128)}, f32[]{:T(128)}, f32[]{:T(128)}) all-reduce(f32[]{:T(128)} %get-tuple-element.20, f32[]{:T(128)} %get-tuple-element.16, f32[]{:T(128)} %get-tuple-element.15, f32[]{:T(128)} %get-tuple-element.19), channel_id=1, replica_groups=mesh['coil'=32,'slab'=8] {'coil','slab'}, use_global_device_ids=true, to_apply=%region_6.7 | all-reduce | flops 4 | bytes 32 | tf_op jit(solution)/shard_map/psum | solution.py:119
  595.3 2.1 fusion.12
  597.4 140.0 %psum.55 = f32[2,32,32]{2,1,0:T(8,128)S(1)} all-reduce(f32[2,32,32]{2,1,0:T(8,128)S(1)} %pad_maximum_fusion.7), channel_id=1, replica_groups=mesh['coil'=32,'slab'=8] {'coil'}, use_global_device_ids=true, to_apply=%region_17.18 | all-reduce | flops 2048 | bytes 16384 | tf_op jit(solution)/shard_map/psum | solution.py:128
  741.3 2.3 fusion.14
  744.7 2.0 fusion.64
  (57 shorter events, 20.2 us)
Async XLA Ops:
  7.2 83.4 %all-gather.4.cloned.1.call-start = ((), (), s32[]{:S(2)}) async-start(), calls=%async_computation.4 | async-start | bytes 1081344 | tf_op jit(solution)/shard_map/all_gather | solution.py:74
  9.4 169.6 %all-gather.8.cloned.1.call-start = ((), (), s32[]{:S(2)}) async-start(), calls=%async_computation.6 | async-start | bytes 1081344 | tf_op jit(solution)/shard_map/all_gather | solution.py:74
  16.2 77.7 %copy-start.3 = (bf16[1,256,2,256]{3,1,0,2:T(8,128)(2,1)}, bf16[1,256,2,256]{3,1,0,2:T(8,128)(2,1)S(1)}, u32[]{:S(2)}) copy-start(bf16[1,256,2,256]{3,1,0,2:T(8,128)(2,1)S(1)} %get-tuple-element.47) | copy-start | bytes 786436
  112.1 6.5 copy-start.8
  112.2 6.6 copy-start.7
  112.2 20.0 %all-to-all-start = ((bf16[8,2,32768]{2,1,0:T(2,128)(2,1)}), bf16[8,2,32768]{2,1,0:T(2,128)(2,1)}, u32[]{:S(2)}, u32[]{:S(2)}) async-start(bf16[8,2,32768]{2,1,0:T(2,128)(2,1)} %reshape.272), calls=%async_computation | async-start | bytes 2097152 | tf_op jit(solution)/shard_map/all_to_all | solution.py:80
  152.0 4.4 copy-start.6
  173.2 20.2 %all-to-all-start.1 = ((bf16[8,2,32768]{2,1,0:T(2,128)(2,1)}), bf16[8,2,32768]{2,1,0:T(2,128)(2,1)}, u32[]{:S(2)}, u32[]{:S(2)}) async-start(bf16[8,2,32768]{2,1,0:T(2,128)(2,1)} %reshape.274), calls=%async_computation.1 | async-start | bytes 2097152 | tf_op jit(solution)/shard_map/all_to_all | solution.py:95
  178.7 189.4 %all-reduce.5.cloned.1.call-start = ((), (), s32[]{:S(2)}) async-start(), calls=%async_computation.7 | async-start | bytes 2097152
  213.4 2.2 copy-start.5
  215.6 1.6 copy-start.1
  219.2 1.7 copy-start.9
  219.2 148.9 %copy-start.4 = (f32[1,2,32,256]{3,2,1,0:T(8,128)S(1)}, f32[1,2,32,256]{3,2,1,0:T(8,128)}, u32[]{:S(2)}) copy-start(f32[1,2,32,256]{3,2,1,0:T(8,128)} %param.6) | copy-start | bytes 196612
  220.8 224.0 %all-gather.6.cloned.1.call-start = ((), (), s32[]{:S(2)}) async-start(), calls=%async_computation.5 | async-start | bytes 1081344 | tf_op jit(solution)/shard_map/all_gather | solution.py:74
  389.2 75.6 %all-to-all-start.3 = ((bf16[8,2,32768]{2,1,0:T(2,128)(2,1)}), bf16[8,2,32768]{2,1,0:T(2,128)(2,1)}, u32[]{:S(2)}, u32[]{:S(2)}) async-start(bf16[8,2,32768]{2,1,0:T(2,128)(2,1)} %reshape.278), calls=%async_computation.3 | async-start | bytes 2097152 | tf_op jit(solution)/shard_map/all_to_all | solution.py:80
  464.8 27.3 %all-to-all-start.2 = ((bf16[8,2,32768]{2,1,0:T(2,128)(2,1)}), bf16[8,2,32768]{2,1,0:T(2,128)(2,1)}, u32[]{:S(2)}, u32[]{:S(2)}) async-start(bf16[8,2,32768]{2,1,0:T(2,128)(2,1)} %reshape.276), calls=%async_computation.2 | async-start | bytes 2097152 | tf_op jit(solution)/shard_map/all_to_all | solution.py:80
  483.3 5.4 copy-start.2
  505.8 6.3 copy-start
Sparse Core Ops, SparseCore 0:
  11.1 79.3 all-gather.3
  93.1 73.8 all-gather.7
  221.0 147.1 all-reduce.4
  371.2 73.5 all-gather.5
where the time goes:
time: 763 us; the launch traced here: 753 us
  blocking collectives  288 us (38%)
  waiting for transfers between devices  219 us (29%)
  local copies, waits for them, and re-layouts  143 us (19%)
  other arithmetic  33.3 us (4%)
  matrix products  27.2 us (4%)
  between operations  21.9 us (3%)
  starting transfers between devices  21.2 us (3%)
    psum x1, blocking collectives, shards(): lax.psum(jnp.stack([line_terms(first_k), line_terms(second_k)]), 'coil')  140 us
    all_gather x3, waiting for transfers between devices, gathered_front(): return front(lax.all_gather(shard, 'coil', axis=0, tiled=True))  125 us
    psum x1, blocking collectives, shards(): lax.psum((jnp.sum(residual * residual), jnp.sum(residual * direction), jn...  74.5 us
    psum x1, blocking collectives, shards(): lax.psum((jnp.sum(direction * direction), jnp.sum(first_w * first_w)), both)  73.8 us
    unnamed x5, waiting for transfers between devices  71.1 us
    unnamed x30, local copies, waits for them, and re-layouts  61.8 us
    all_to_all x6, local copies, waits for them, and re-layouts, to_kspace(): lax.all_to_all(mixed, 'slab', split_axis=3, concat_axis=2, tiled=True)  38 us
    convert_element_type x3, local copies, waits for them, and re-layouts, to_kspace(): mixed = jnp.einsum('nixk,inom->moxk', rows, z_fwd, preferred_element_type...  21 us
  transfers between devices with their start and end apart: 8, of which 5 were waited for; matrix products, arithmetic and copies ran while one was open for 18% of the time, Pallas kernels for 0%

commit v1 on v0

--- a/solution.py
+++ b/solution.py
@@ -125,7 +125,9 @@
         ),
         both,
     )
-    lines = lax.psum(jnp.stack([line_terms(first_k), line_terms(second_k)]), "coil")
+    lines = jnp.sum(
+        lax.all_gather(jnp.stack([line_terms(first_k), line_terms(second_k)]), "coil"), axis=0
+    )
     beta = norm_next / norm_now
     curvature = (
         second_energy

time: 763 us -> 677 us (0.89)
  blocking collectives: 288 us -> 201 us
    psum x1 -> x0, blocking collectives: 140 us -> none  [shards(): lax.psum(jnp.stack([line_terms(first_k), line_terms(second_k)]), 'coil')]
    all_gather x0 -> x1, blocking collectives: none -> 53.1 us  [shards(): lax.all_gather(jnp.stack([line_terms(first_k), line_terms(second_k)]), 'c...]
  transfers between devices with their start and end apart: 8 -> 8, of which waited for: 5 -> 5; matrix products, arithmetic and copies ran while one was open for 18% -> 20% of each run, Pallas kernels for 0% -> 0%
where the time goes in v1:
time: 677 us; the launch traced here: 668 us
  waiting for transfers between devices  219 us (32%)
  blocking collectives  201 us (30%)
  local copies, waits for them, and re-layouts  143 us (21%)
  other arithmetic  34.6 us (5%)
  matrix products  27.2 us (4%)
  between operations  21.9 us (3%)
  starting transfers between devices  21.2 us (3%)
    all_gather x3, waiting for transfers between devices, gathered_front(): return front(lax.all_gather(shard, 'coil', axis=0, tiled=True))  125 us
    psum x1, blocking collectives, shards(): lax.psum((jnp.sum(residual * residual), jnp.sum(residual * direction), jn...  74.5 us
    psum x1, blocking collectives, shards(): lax.psum((jnp.sum(direction * direction), jnp.sum(first_w * first_w)), both)  73.8 us
    unnamed x5, waiting for transfers between devices  71.1 us
    unnamed x30, local copies, waits for them, and re-layouts  61.8 us
    all_gather x1, blocking collectives, shards(): lax.all_gather(jnp.stack([line_terms(first_k), line_terms(second_k)]), 'c...  53.1 us
    all_to_all x6, local copies, waits for them, and re-layouts, to_kspace(): lax.all_to_all(mixed, 'slab', split_axis=3, concat_axis=2, tiled=True)  38 us
    convert_element_type x3, local copies, waits for them, and re-layouts, to_kspace(): mixed = jnp.einsum('nixk,inom->moxk', rows, z_fwd, preferred_element_type...  21 us
  transfers between devices with their start and end apart: 8, of which 5 were waited for; matrix products, arithmetic and copies ran while one was open for 20% of the time, Pallas kernels for 0%

profile of v1, /device:TPU:2, one launch (start us, length us, event | category | flops | bytes accessed | tf_op | source)
XLA Modules:
  0.0 667.9 jit_solution(2360762838258197628)
XLA Ops:
  7.2 2.1 fusion.89
  14.3 1.8 bitcast_convert_fusion.8
  16.2 74.3 %all-gather.5.cloned.1.call-done = bf16[32,2,32,256]{3,2,1,0:T(8,128)(2,1)} async-done(((bf16[1,2,32,256]{3,2,1,0:T(8,128)(2,1)}), bf16[32,2,32,256]{3,2,1,0:T(8,128)(2,1)}) %all-gather.5.cloned.1.call-update) | async-done | bytes 1048592 | tf_op jit(solution)/shard_map/all_gather | solution.py:74
  90.6 1.8 copy_convert_fusion.2
  93.9 3.2 fusion.4
  97.1 7.2 %copy.81 = bf16[32,2,32,256]{0,2,1,3:T(8,128)(2,1)} copy(bf16[32,2,32,256]{3,0,2,1:T(8,128)(2,1)} %fusion.4) | data formatting | bytes 2097152 | tf_op jit(solution)/shard_map/convert_element_type | solution.py:79
  104.3 7.8 %reshape.273 = bf16[8,2,32768]{2,1,0:T(2,128)(2,1)} reshape(bf16[256,2,32,32]{3,2,1,0:T(8,128)(2,1)} %bitcast.297) | data formatting | bytes 2097152
  112.2 5.5 all-to-all-start
  120.4 11.7 %all-to-all-done = bf16[8,2,32768]{2,1,0:T(2,128)(2,1)} async-done(((bf16[8,2,32768]{2,1,0:T(2,128)(2,1)}), bf16[8,2,32768]{2,1,0:T(2,128)(2,1)}, u32[]{:S(2)}, u32[]{:S(2)}) %all-to-all-start) | async-done | bytes 1048608 | tf_op jit(solution)/shard_map/all_to_all | solution.py:80
  132.1 7.0 %reshape.274 = bf16[256,2,32,32]{3,2,1,0:T(8,128)(2,1)} reshape(bf16[8,2,32768]{2,1,0:T(2,128)(2,1)} %all-to-all-done) | data formatting | bytes 2097152
  139.1 6.7 %copy.82 = bf16[32,2,32,8,32]{2,3,4,1,0:T(8,128)(2,1)} copy(bf16[32,2,32,8,32]{0,2,1,4,3:T(8,128)(2,1)} %bitcast.301) | data formatting | bytes 2097152 | tf_op jit(solution)/shard_map/all_to_all | solution.py:80
  145.9 6.2 reshape.244
  152.0 4.4 fusion.2
  158.1 7.2 %copy.85 = bf16[32,2,256,32]{3,0,1,2:T(8,128)(2,1)} copy(bf16[32,2,256,32]{2,3,0,1:T(8,128)(2,1)} %fusion.9) | data formatting | bytes 2097152 | tf_op jit(solution)/shard_map/convert_element_type | solution.py:94
  165.3 7.8 %reshape.275 = bf16[8,2,32768]{2,1,0:T(2,128)(2,1)} reshape(bf16[256,2,32,32]{3,2,1,0:T(8,128)(2,1)} %bitcast.298) | data formatting | bytes 2097152
  173.2 5.6 all-to-all-start.1
  178.9 3.2 copy_convert_fusion
  182.1 11.2 %all-to-all-done.1 = bf16[8,2,32768]{2,1,0:T(2,128)(2,1)} async-done(((bf16[8,2,32768]{2,1,0:T(2,128)(2,1)}), bf16[8,2,32768]{2,1,0:T(2,128)(2,1)}, u32[]{:S(2)}, u32[]{:S(2)}) %all-to-all-start.1) | async-done | bytes 1048608 | tf_op jit(solution)/shard_map/all_to_all | solution.py:95
  193.3 7.0 %reshape.276 = bf16[256,2,32,32]{3,2,1,0:T(8,128)(2,1)} reshape(bf16[8,2,32768]{2,1,0:T(2,128)(2,1)} %all-to-all-done.1) | data formatting | bytes 2097152
  200.4 6.9 %copy.160 = bf16[32,2,8,32,32]{4,2,3,1,0:T(8,128)(2,1)} copy(bf16[32,2,8,32,32]{4,0,1,3,2:T(8,128)(2,1)} %bitcast.303) | data formatting | bytes 2097152 | tf_op jit(solution)/shard_map/all_to_all | solution.py:95
  207.2 6.2 all_to_all.59
  213.4 2.2 fusion.5
  217.2 1.9 subtract_convert_fusion
  221.5 73.8 %all-reduce.2 = (f32[]{:T(128)}, f32[]{:T(128)}) all-reduce(f32[]{:T(128)} %get-tuple-element.49, f32[]{:T(128)} %get-tuple-element.40), channel_id=1, replica_groups=mesh['coil'=32,'slab'=8] {'coil','slab'}, use_global_device_ids=true, to_apply=%region_1.2 | all-reduce | flops 2 | bytes 16 | tf_op jit(solution)/shard_map/psum | solution.py:88
  297.2 71.0 %all-reduce.5.cloned.1.call-done = bf16[32,2,32,256]{3,2,0,1:T(8,128)(2,1)} async-done(((bf16[32,2,32,256]{3,2,0,1:T(8,128)(2,1)}), bf16[32,2,32,256]{3,2,0,1:T(8,128)(2,1)}) %all-reduce.5.cloned.1.call-update) | async-done | bytes 1048592
  368.2 2.7 fusion.61
  370.9 3.3 fusion.7
  374.1 7.2 %copy.103 = bf16[32,2,32,256]{0,2,1,3:T(8,128)(2,1)} copy(bf16[32,2,32,256]{3,0,2,1:T(8,128)(2,1)} %fusion.7) | data formatting | bytes 2097152 | tf_op jit(solution)/shard_map/convert_element_type | solution.py:79
  381.4 7.8 %reshape.279 = bf16[8,2,32768]{2,1,0:T(2,128)(2,1)} reshape(bf16[256,2,32,32]{3,2,1,0:T(8,128)(2,1)} %bitcast.299) | data formatting | bytes 2097152
  389.2 5.1 all-to-all-start.3
  394.3 50.5 %all-gather.7.cloned.1.call-done = bf16[32,2,32,256]{3,2,1,0:T(8,128)(2,1)} async-done(((bf16[1,2,32,256]{3,2,1,0:T(8,128)(2,1)}), bf16[32,2,32,256]{3,2,1,0:T(8,128)(2,1)}) %all-gather.7.cloned.1.call-update) | async-done | bytes 1048592 | tf_op jit(solution)/shard_map/all_gather | solution.py:74
  448.2 2.3 fusion.6
  450.5 6.5 copy.97
  457.0 7.8 %reshape.277 = bf16[8,2,32768]{2,1,0:T(2,128)(2,1)} reshape(bf16[256,2,32,32]{3,2,1,0:T(8,128)(2,1)} %bitcast.300) | data formatting | bytes 2097152
  464.8 4.8 all-to-all-start.2
  469.6 7.0 %reshape.280 = bf16[256,2,32,32]{3,2,1,0:T(8,128)(2,1)} reshape(bf16[8,2,32768]{2,1,0:T(2,128)(2,1)} %all-to-all-done.3) | data formatting | bytes 2097152
  476.6 6.7 %copy.104 = bf16[32,2,32,8,32]{2,3,4,1,0:T(8,128)(2,1)} copy(bf16[32,2,32,8,32]{0,2,1,4,3:T(8,128)(2,1)} %bitcast.305) | data formatting | bytes 2097152 | tf_op jit(solution)/shard_map/all_to_all | solution.py:80
  483.3 5.4 reshape.265
  488.7 3.4 fusion
  492.1 7.0 %reshape.278 = bf16[256,2,32,32]{3,2,1,0:T(8,128)(2,1)} reshape(bf16[8,2,32768]{2,1,0:T(2,128)(2,1)} %all-to-all-done.2) | data formatting | bytes 2097152
  499.1 6.7 %copy.98 = bf16[32,2,32,8,32]{2,3,4,1,0:T(8,128)(2,1)} copy(bf16[32,2,32,8,32]{0,2,1,4,3:T(8,128)(2,1)} %bitcast.307) | data formatting | bytes 2097152 | tf_op jit(solution)/shard_map/all_to_all | solution.py:80
  505.8 6.3 reshape.259
  512.1 6.2 multiply_reduce_fusion
  518.3 74.5 %all-reduce.1 = (f32[]{:T(128)}, f32[]{:T(128)}, f32[]{:T(128)}, f32[]{:T(128)}) all-reduce(f32[]{:T(128)} %get-tuple-element.20, f32[]{:T(128)} %get-tuple-element.16, f32[]{:T(128)} %get-tuple-element.15, f32[]{:T(128)} %get-tuple-element.19), channel_id=1, replica_groups=mesh['coil'=32,'slab'=8] {'coil','slab'}, use_global_device_ids=true, to_apply=%region_6.7 | all-reduce | flops 4 | bytes 32 | tf_op jit(solution)/shard_map/psum | solution.py:119
  595.3 2.1 fusion.12
  597.4 53.1 %all-gather = f32[64,32,32]{2,1,0:T(8,128)} all-gather(f32[2,32,32]{2,1,0:T(8,128)S(1)} %pad_maximum_fusion.7), channel_id=2, replica_groups=mesh['coil'=32,'slab'=8] {'coil'}, dimensions={0}, use_global_device_ids=true | all-gather | bytes 270336 | tf_op jit(solution)/shard_map/all_gather | solution.py:129
  655.8 2.3 fusion.14
  659.1 2.0 fusion.64
  (58 shorter events, 21.6 us)
Async XLA Ops:
  7.2 83.4 %all-gather.5.cloned.1.call-start = ((), (), s32[]{:S(2)}) async-start(), calls=%async_computation.4 | async-start | bytes 1081344 | tf_op jit(solution)/shard_map/all_gather | solution.py:74
  9.4 169.6 %all-gather.9.cloned.1.call-start = ((), (), s32[]{:S(2)}) async-start(), calls=%async_computation.6 | async-start | bytes 1081344 | tf_op jit(solution)/shard_map/all_gather | solution.py:74
  16.2 77.7 %copy-start.3 = (bf16[1,256,2,256]{3,1,0,2:T(8,128)(2,1)}, bf16[1,256,2,256]{3,1,0,2:T(8,128)(2,1)S(1)}, u32[]{:S(2)}) copy-start(bf16[1,256,2,256]{3,1,0,2:T(8,128)(2,1)S(1)} %get-tuple-element.47) | copy-start | bytes 786436
  112.1 6.5 copy-start.8
  112.2 6.6 copy-start.7
  112.2 20.0 %all-to-all-start = ((bf16[8,2,32768]{2,1,0:T(2,128)(2,1)}), bf16[8,2,32768]{2,1,0:T(2,128)(2,1)}, u32[]{:S(2)}, u32[]{:S(2)}) async-start(bf16[8,2,32768]{2,1,0:T(2,128)(2,1)} %reshape.273), calls=%async_computation | async-start | bytes 2097152 | tf_op jit(solution)/shard_map/all_to_all | solution.py:80
  152.0 4.4 copy-start.6
  173.2 20.2 %all-to-all-start.1 = ((bf16[8,2,32768]{2,1,0:T(2,128)(2,1)}), bf16[8,2,32768]{2,1,0:T(2,128)(2,1)}, u32[]{:S(2)}, u32[]{:S(2)}) async-start(bf16[8,2,32768]{2,1,0:T(2,128)(2,1)} %reshape.275), calls=%async_computation.1 | async-start | bytes 2097152 | tf_op jit(solution)/shard_map/all_to_all | solution.py:95
  178.7 189.4 %all-reduce.5.cloned.1.call-start = ((), (), s32[]{:S(2)}) async-start(), calls=%async_computation.7 | async-start | bytes 2097152
  213.4 2.2 copy-start.5
  215.6 1.6 copy-start.1
  219.2 1.7 copy-start.9
  219.2 148.9 %copy-start.4 = (f32[1,2,32,256]{3,2,1,0:T(8,128)S(1)}, f32[1,2,32,256]{3,2,1,0:T(8,128)}, u32[]{:S(2)}) copy-start(f32[1,2,32,256]{3,2,1,0:T(8,128)} %param.6) | copy-start | bytes 196612
  220.8 224.0 %all-gather.7.cloned.1.call-start = ((), (), s32[]{:S(2)}) async-start(), calls=%async_computation.5 | async-start | bytes 1081344 | tf_op jit(solution)/shard_map/all_gather | solution.py:74
  389.2 75.6 %all-to-all-start.3 = ((bf16[8,2,32768]{2,1,0:T(2,128)(2,1)}), bf16[8,2,32768]{2,1,0:T(2,128)(2,1)}, u32[]{:S(2)}, u32[]{:S(2)}) async-start(bf16[8,2,32768]{2,1,0:T(2,128)(2,1)} %reshape.279), calls=%async_computation.3 | async-start | bytes 2097152 | tf_op jit(solution)/shard_map/all_to_all | solution.py:80
  464.8 27.3 %all-to-all-start.2 = ((bf16[8,2,32768]{2,1,0:T(2,128)(2,1)}), bf16[8,2,32768]{2,1,0:T(2,128)(2,1)}, u32[]{:S(2)}, u32[]{:S(2)}) async-start(bf16[8,2,32768]{2,1,0:T(2,128)(2,1)} %reshape.277), calls=%async_computation.2 | async-start | bytes 2097152 | tf_op jit(solution)/shard_map/all_to_all | solution.py:80
  483.3 5.4 copy-start.2
  505.8 6.3 copy-start
Sparse Core Ops, SparseCore 0:
  11.1 79.3 all-gather.4
  93.1 73.8 all-gather.8
  221.0 147.1 all-reduce.4
  371.2 73.5 all-gather.6
